TPU v7x, 768 devices: a whole 4x8x12 slice. The times are simulated.
768 devices in a mesh: gx: 12 (over z), gy: 64 (over y, x, core).
Axes of the slice: x: 4, y: 8, z: 12, core: 2. Of those that a mesh axis runs over, the one named last changes fastest.
Arguments:
- heat_source: float32 [8, 192, 49152], P(None, 'gx', 'gy'), may hold values from -90 to 90
- density: float32 [192, 49152], P('gx', 'gy'), may hold values from 0.3 to 1
Outputs:
- solution_field: float32 [8, 192, 49152], P(None, 'gx', 'gy')
- residual: float32 [8, 192, 49152], P(None, 'gx', 'gy')
All inputs are finite; a program needn't handle non-finite values.
Results may differ from a plain program's by a relative error of at most 0.0003.
Values sent between devices are 32-bit elements; how exact they have to be, the bound alone decides.
A program may use at most 32 MiB of HBM per device.

v0:
```python
import jax
import jax.numpy as jnp
import numpy as np
from jax import lax
from jax.sharding import PartitionSpec as P

NZ = 96
ITERS = 2


KMIN = 0.001


def from_behind(shard, axis, by):
    length = lax.axis_size(axis)
    pairs = [(i, i + by) for i in range(length) if 0 <= i + by < length]
    return lax.ppermute(shard, axis, pairs)


def with_halo(block, sides, width):
    for axis, dim in sides:
        count = lax.axis_size(axis)
        forward = [(i, i + 1) for i in range(count - 1)]
        backward = [(target, source) for source, target in forward]
        low = lax.ppermute(
            lax.slice_in_dim(block, block.shape[dim] - width, None, axis=dim), axis, forward
        )
        high = lax.ppermute(lax.slice_in_dim(block, 0, width, axis=dim), axis, backward)
        block = jnp.concatenate([low, block, high], axis=dim)
    return block


def stiffness():
    table = np.zeros((8, 8), np.float32)
    levels = [4.0, 0.0, -1.0, -1.0]
    for first in range(8):
        for second in range(8):
            differ = first ^ second
            apart = (differ & 1) + (differ >> 1 & 1) + (differ >> 2 & 1)
            table[first, second] = levels[apart] / 12.0
    return table


def corners():
    return [(corner >> 2 & 1, corner >> 1 & 1, corner & 1) for corner in range(8)]


def conductance(density):
    return KMIN + (1.0 - KMIN) * (density * density * density)


def upper_masks(length):
    keep_z = (jnp.arange(length) % NZ < NZ - 1).astype(jnp.float32)
    ones = jnp.ones((length,), jnp.float32)
    picked = [keep_z if off_z else ones for off_x, off_y, off_z in corners()]
    return jnp.stack(picked)[:, None, None, :]


def spread_nodes(elems, rows, out_len):
    padded = jnp.pad(elems, ((0, 0), (0, 0), (0, 0), (1, 0)))
    summed = None
    for corner, (off_x, off_y, off_z) in enumerate(corners()):
        start_at = (1 - off_y) * NZ - off_z + 1
        piece = padded[corner, :, 1 - off_x : 1 - off_x + rows, start_at : start_at + out_len]
        summed = piece if summed is None else summed + piece
    return summed


def block_apply(extended, conduct_blk, rows, cols, k_elem):
    elem_len = (cols + 1) * NZ
    masks = upper_masks(elem_len)
    extended = jnp.pad(extended, ((0, 0), (0, 0), (0, 1)))
    corner_vals = (
        jnp.stack(
            [
                extended[
                    :, off_x : off_x + rows + 1, off_y * NZ + off_z : off_y * NZ + off_z + elem_len
                ]
                for off_x, off_y, off_z in corners()
            ]
        )
        * masks
    )
    elems = (
        jnp.einsum("nm,mlag->nlag", k_elem, corner_vals, precision=lax.Precision.HIGHEST)
        * conduct_blk
        * masks
    )
    return spread_nodes(elems, rows, cols * NZ)


def node_weights(conduct_blk, rows, cols, k_elem):
    elem_len = (cols + 1) * NZ
    masks = upper_masks(elem_len)
    weights = jnp.broadcast_to(conduct_blk * k_elem[0, 0], (8, 1, rows + 1, elem_len)) * masks
    return spread_nodes(weights, rows, cols * NZ)


def local_sums(first, second):
    return jnp.sum(first * second, axis=(1, 2))


def residual_dot(residual, scaled):
    return lax.psum(local_sums(residual, scaled), ("gx", "gy"))


def per_device(heat_source, density):
    load_count, x_cells, flat_len = heat_source.shape
    y_cells = flat_len // NZ
    conduct = conductance(density)
    k_elem = jnp.asarray(stiffness())
    row_in = from_behind(conduct[x_cells - 1 :], "gx", 1)
    conduct_x = jnp.concatenate([row_in, conduct], 0).reshape(x_cells + 1, y_cells, NZ)
    col_in = from_behind(conduct_x[:, y_cells - 1 :], "gy", 1)
    conduct_e = jnp.concatenate([col_in, conduct_x], 1).reshape(x_cells + 1, (y_cells + 1) * NZ)
    precond_whole = node_weights(conduct_e, x_cells, y_cells, k_elem)

    def precond_at():
        return precond_whole

    start_cycle = 0
    solution = jnp.zeros_like(heat_source)
    cycle = start_cycle
    residual = heat_source
    scaled = residual / precond_at()
    direction = scaled
    rz_sum = residual_dot(residual, scaled)
    for step in range(ITERS):
        blocks = direction.reshape(load_count, x_cells, y_cells, NZ)
        extended = with_halo(blocks, (("gx", 1), ("gy", 2)), 1)
        extended = extended.reshape(load_count, x_cells + 2, (y_cells + 2) * NZ)
        image = block_apply(extended, conduct_e, x_cells, y_cells, k_elem)
        next_cycle = cycle
        owned_dir = direction
        curvature = lax.psum(local_sums(owned_dir, image), ("gx", "gy"))
        alpha = (rz_sum / curvature)[:, None, None]
        solution = solution + alpha * owned_dir
        residual = residual - alpha * image
        cycle = next_cycle
        if step + 1 < ITERS:
            scaled = residual / precond_at()
            rz_next = residual_dot(residual, scaled)
            direction = scaled + (rz_next / rz_sum)[:, None, None] * direction
            rz_sum = rz_next
    return (solution, residual)


def solution(mesh):
    placed = (P(None, "gx", "gy"), P("gx", "gy"))
    return jax.shard_map(
        per_device,
        mesh=mesh,
        in_specs=placed,
        out_specs=(P(None, "gx", "gy"), P(None, "gx", "gy")),
        check_vma=False,
    )
```

profile of v0, /device:TPU:1, one launch (start us, length us, event | category | flops | bytes accessed | tf_op | source)
XLA Modules:
  0.0 413.8 jit_solution(939601505650247891)
XLA Ops:
  0.6 0.8 fusion.37
  1.5 4.8 %collective-permute-start = (f32[1,768]{1,0:T(1,128)S(1)}, f32[1,768]{1,0:T(1,128)S(1)}, u32[]{:S(2)}, u32[]{:S(2)}) collective-permute-start(f32[1,768]{1,0:T(1,128)S(1)} %slice.234), channel_id=1, source_target_pairs={{0,64},{64,128},{128,192},{192,256},{256,320},{320,384},{384,448},... | collective-permute-start | bytes 9224 | tf_op jit(solution)/shard_map/ppermute | solution.py:17
  6.3 0.7 collective-permute-done
  7.1 4.5 %collective-permute-start.1 = (f32[17,1,96]{2,1,0:T(1,128)S(1)}, f32[17,1,96]{2,1,0:T(1,128)S(1)}, u32[]{:S(2)}, u32[]{:S(2)}) collective-permute-start(f32[17,1,96]{2,1,0:T(1,128)S(1)} %slice.235), channel_id=1, source_target_pairs={{0,1},{1,2},{2,3},{3,4},{4,5},{5,6},{6,7},{7,8},{8,9},{9,10},{10,1... | collective-permute-start | bytes 19592 | tf_op jit(solution)/shard_map/ppermute | solution.py:17
  11.8 4.8 %collective-permute-done.1 = f32[17,1,96]{2,1,0:T(1,128)S(1)} collective-permute-done((f32[17,1,96]{2,1,0:T(1,128)S(1)}, f32[17,1,96]{2,1,0:T(1,128)S(1)}, u32[]{:S(2)}, u32[]{:S(2)}) %collective-permute-start.1) | collective-permute-done | bytes 6560 | tf_op jit(solution)/shard_map/ppermute | solution.py:17
  16.9 1.0 broadcast_divide_fusion
  18.0 0.3 reshape.130
  18.3 3.9 collective-permute-start.2
  22.2 1.3 collective-permute-start.3
  23.6 3.3 collective-permute-done.3
  27.0 1.9 collective-permute-start.4
  28.9 2.9 collective-permute-start.5
  31.8 2.8 collective-permute-done.5
  34.6 0.3 pad_maximum_fusion
  34.8 0.4 reshape.131
  35.2 0.4 copy.13
  35.6 0.2 fusion.22
  35.9 0.2 fusion.21
  36.1 0.2 fusion.5
  36.4 0.2 fusion.19
  36.7 0.2 fusion.18
  36.9 0.2 fusion.7
  37.2 0.4 broadcast_multiply_fusion.1
  37.9 5.8 %bitcast_multiply_fusion.1 = f32[8,8,17,864]{3,0,2,1:T(8,128)S(1)} fusion(f32[8,864]{1,0:T(8,128)S(1)} %stack.71, f32[17,864]{1,0:T(8,128)S(1)} %reshape.129, f32[8,8,1,1]{1,0,3,2:T(8,128)S(1)} %copy-done.1, f32[8,8,17,864]{3,2,1,0:T(8,128)S(1)} %broadcast_multiply_fusion.1), kind=kOutput, calls=%fused_computation.4 | convolution fusion | flops 92123136 | bytes 7606912 | tf_op jit(solution)/shard_map/nm,mlag->nlag/dot_general | solution.py:85
  43.7 5.2 %fusion.25 = f32[1,8,16,768]{3,0,2,1:T(1,128)S(1)} fusion(f32[8,8,17,864]{3,0,2,1:T(8,128)S(1)} %bitcast_multiply_fusion.1), kind=kLoop, calls=%fused_computation.54 | loop fusion | flops 688128 | bytes 6651904 | tf_op jit(solution)/shard_map/add | solution.py:65
  49.1 120.2 %all-reduce.5 = (f32[8]{0:T(128)S(1)}, f32[8]{0:T(128)S(1)}) all-reduce(f32[8]{0:T(128)S(1)} %get-tuple-element.3, f32[8]{0:T(128)S(1)} %get-tuple-element.2), channel_id=1, replica_groups=mesh['gx'=12,'gy'=64] {'gx','gy'}, use_global_device_ids=true, to_apply=%region_1.2 | all-reduce | flops 16 | bytes 128 | tf_op jit(solution)/shard_map/psum | solution.py:104
  169.6 103.9 %psum.30 = f32[8]{0:T(128)S(1)} all-reduce(f32[8]{0:T(128)S(1)} %get-tuple-element.8), channel_id=1, replica_groups=mesh['gx'=12,'gy'=64] {'gx','gy'}, use_global_device_ids=true, to_apply=%region_5.6 | all-reduce | flops 8 | bytes 64 | tf_op jit(solution)/shard_map/psum | solution.py:104
  273.6 0.3 reshape.132
  273.9 3.7 collective-permute-start.6
  277.5 1.3 collective-permute-start.7
  278.9 3.3 collective-permute-done.7
  282.3 5.6 %collective-permute-start.8 = (f32[8,18,1,96]{3,2,0,1:T(1,128)S(1)}, f32[8,18,1,96]{3,2,0,1:T(1,128)S(1)}, u32[]{:S(2)}, u32[]{:S(2)}) collective-permute-start(f32[8,18,1,96]{3,2,0,1:T(1,128)S(1)} %get-tuple-element.10), channel_id=1, source_target_pairs={{0,1},{1,2},{2,3},{3,4},{4,5},{5,6},{6,7},{7,8},{8,9},{9,10},{10,1... | collective-permute-start | bytes 165896 | tf_op jit(solution)/shard_map/ppermute | solution.py:25
  287.9 1.9 collective-permute-start.9
  289.9 3.7 collective-permute-done.9
  293.6 0.3 pad_maximum_fusion.1
  293.9 0.4 reshape.133
  294.2 0.4 copy.26
  294.9 0.2 fusion.15
  295.1 0.2 fusion.9
  295.5 0.2 fusion.13
  295.7 0.2 fusion.12
  296.0 0.2 fusion.11
  296.2 0.4 broadcast_multiply_fusion
  296.7 6.1 %fusion = f32[8,17,864,8]{2,3,1,0:T(8,128)S(1)} fusion(f32[8,8,1,1]{1,0,3,2:T(8,128)S(1)} %copy-done.1, f32[8,8,17,864]{3,2,1,0:T(8,128)S(1)} %broadcast_multiply_fusion), kind=kOutput, calls=%fused_computation.5 | convolution fusion | flops 90243072 | bytes 7520512 | tf_op jit(solution)/shard_map/nm,mlag->nlag/dot_general | solution.py:85
  302.7 0.9 bitcast_multiply_fusion
  303.6 0.8 fusion.34
  304.4 108.4 %psum.31 = f32[8]{0:T(128)S(1)} all-reduce(f32[8]{0:T(128)S(1)} %get-tuple-element.6), channel_id=1, replica_groups=mesh['gx'=12,'gy'=64] {'gx','gy'}, use_global_device_ids=true, to_apply=%region_7.8 | all-reduce | flops 8 | bytes 64 | tf_op jit(solution)/shard_map/psum | solution.py:135
  412.8 1.0 fusion.35
  (45 shorter events, 2.1 us)
Async XLA Ops:
  1.5 5.5 %collective-permute-start = (f32[1,768]{1,0:T(1,128)S(1)}, f32[1,768]{1,0:T(1,128)S(1)}, u32[]{:S(2)}, u32[]{:S(2)}) collective-permute-start(f32[1,768]{1,0:T(1,128)S(1)} %slice.234), channel_id=1, source_target_pairs={{0,64},{64,128},{128,192},{192,256},{256,320},{320,384},{384,448},... | collective-permute-start | bytes 9224 | tf_op jit(solution)/shard_map/ppermute | solution.py:17
  7.1 9.5 %collective-permute-start.1 = (f32[17,1,96]{2,1,0:T(1,128)S(1)}, f32[17,1,96]{2,1,0:T(1,128)S(1)}, u32[]{:S(2)}, u32[]{:S(2)}) collective-permute-start(f32[17,1,96]{2,1,0:T(1,128)S(1)} %slice.235), channel_id=1, source_target_pairs={{0,1},{1,2},{2,3},{3,4},{4,5},{5,6},{6,7},{7,8},{8,9},{9,10},{10,1... | collective-permute-start | bytes 19592 | tf_op jit(solution)/shard_map/ppermute | solution.py:17
  18.3 5.2 %collective-permute-start.2 = (f32[8,1,8,96]{3,2,0,1:T(8,128)S(1)}, f32[8,1,8,96]{3,2,0,1:T(8,128)S(1)}, u32[]{:S(2)}, u32[]{:S(2)}) collective-permute-start(f32[8,1,8,96]{3,2,0,1:T(8,128)S(1)} %copy.51), channel_id=1, source_target_pairs={{0,64},{64,128},{128,192},{192,256},{256,320},{320,384},{384,448},... | collective-permute-start | bytes 73736 | tf_op jit(solution)/shard_map/ppermute | solution.py:25
  22.2 4.7 %collective-permute-start.3 = (f32[8,1,8,96]{3,2,0,1:T(8,128)S(1)}, f32[8,1,8,96]{3,2,0,1:T(8,128)S(1)}, u32[]{:S(2)}, u32[]{:S(2)}) collective-permute-start(f32[8,1,8,96]{3,2,0,1:T(8,128)S(1)} %copy.52), channel_id=1, source_target_pairs={{64,0},{128,64},{192,128},{256,192},{320,256},{384,320},{448,384},... | collective-permute-start | bytes 73736 | tf_op jit(solution)/shard_map/ppermute | solution.py:28
  27.0 4.8 %collective-permute-start.4 = (f32[8,18,1,96]{3,2,0,1:T(1,128)S(1)}, f32[8,18,1,96]{3,2,0,1:T(1,128)S(1)}, u32[]{:S(2)}, u32[]{:S(2)}) collective-permute-start(f32[8,18,1,96]{3,2,0,1:T(1,128)S(1)} %get-tuple-element.12), channel_id=1, source_target_pairs={{0,1},{1,2},{2,3},{3,4},{4,5},{5,6},{6,7},{7,8},{8,9},{9,10},{10,1... | collective-permute-start | bytes 165896 | tf_op jit(solution)/shard_map/ppermute | solution.py:25
  28.9 5.7 %collective-permute-start.5 = (f32[8,18,1,96]{3,2,0,1:T(1,128)S(1)}, f32[8,18,1,96]{3,2,0,1:T(1,128)S(1)}, u32[]{:S(2)}, u32[]{:S(2)}) collective-permute-start(f32[8,18,1,96]{3,2,0,1:T(1,128)S(1)} %get-tuple-element.13), channel_id=1, source_target_pairs={{1,0},{2,1},{3,2},{4,3},{5,4},{6,5},{7,6},{8,7},{9,8},{10,9},{11,1... | collective-permute-start | bytes 165896 | tf_op jit(solution)/shard_map/ppermute | solution.py:28
  37.2 0.7 copy-start.1
  37.9 11.0 %copy-start = (f32[8,16,768]{2,1,0:T(8,128)S(1)}, f32[8,16,768]{2,1,0:T(8,128)}, u32[]{:S(2)}) copy-start(f32[8,16,768]{2,1,0:T(8,128)} %param.3) | copy-start | bytes 1179652
  273.9 5.0 %collective-permute-start.6 = (f32[8,1,8,96]{3,2,0,1:T(8,128)S(1)}, f32[8,1,8,96]{3,2,0,1:T(8,128)S(1)}, u32[]{:S(2)}, u32[]{:S(2)}) collective-permute-start(f32[8,1,8,96]{3,2,0,1:T(8,128)S(1)} %copy.53), channel_id=1, source_target_pairs={{0,64},{64,128},{128,192},{192,256},{256,320},{320,384},{384,448},... | collective-permute-start | bytes 73736 | tf_op jit(solution)/shard_map/ppermute | solution.py:25
  277.5 4.7 %collective-permute-start.7 = (f32[8,1,8,96]{3,2,0,1:T(8,128)S(1)}, f32[8,1,8,96]{3,2,0,1:T(8,128)S(1)}, u32[]{:S(2)}, u32[]{:S(2)}) collective-permute-start(f32[8,1,8,96]{3,2,0,1:T(8,128)S(1)} %copy.54), channel_id=1, source_target_pairs={{64,0},{128,64},{192,128},{256,192},{320,256},{384,320},{448,384},... | collective-permute-start | bytes 73736 | tf_op jit(solution)/shard_map/ppermute | solution.py:28
  282.3 7.6 %collective-permute-start.8 = (f32[8,18,1,96]{3,2,0,1:T(1,128)S(1)}, f32[8,18,1,96]{3,2,0,1:T(1,128)S(1)}, u32[]{:S(2)}, u32[]{:S(2)}) collective-permute-start(f32[8,18,1,96]{3,2,0,1:T(1,128)S(1)} %get-tuple-element.10), channel_id=1, source_target_pairs={{0,1},{1,2},{2,3},{3,4},{4,5},{5,6},{6,7},{7,8},{8,9},{9,10},{10,1... | collective-permute-start | bytes 165896 | tf_op jit(solution)/shard_map/ppermute | solution.py:25
  287.9 5.7 %collective-permute-start.9 = (f32[8,18,1,96]{3,2,0,1:T(1,128)S(1)}, f32[8,18,1,96]{3,2,0,1:T(1,128)S(1)}, u32[]{:S(2)}, u32[]{:S(2)}) collective-permute-start(f32[8,18,1,96]{3,2,0,1:T(1,128)S(1)} %get-tuple-element.11), channel_id=1, source_target_pairs={{1,0},{2,1},{3,2},{4,3},{5,4},{6,5},{7,6},{8,7},{9,8},{10,9},{11,1... | collective-permute-start | bytes 165896 | tf_op jit(solution)/shard_map/ppermute | solution.py:28
where the time goes:
time: 419 us; the launch traced here: 414 us
  blocking collectives  332 us (79%)
  starting transfers between devices  31.8 us (8%)
  waiting for transfers between devices  18.6 us (4%)
  other arithmetic  12 us (3%)
  matrix products  11.9 us (3%)
  local copies, waits for them, and re-layouts  5.97 us (1%)
    psum x2, blocking collectives, residual_dot(): return lax.psum(local_sums(residual, scaled), ('gx', 'gy'))  224 us
    psum x1, blocking collectives, per_device(): curvature = lax.psum(local_sums(owned_dir, image), ('gx', 'gy'))  108 us
    ppermute x4, starting transfers between devices, with_halo(): lax.ppermute(lax.slice_in_dim(block, block.shape[dim] - width, None, axis...  15.1 us
    ppermute x4, waiting for transfers between devices, with_halo(): lax.ppermute(lax.slice_in_dim(block, 0, width, axis=dim), axis, backward)  13.1 us
    dot_general x2, matrix products, block_apply(): jnp.einsum('nm,mlag->nlag', k_elem, corner_vals, precision=lax.Precision....  11.9 us
    ppermute x2, starting transfers between devices, from_behind(): return lax.ppermute(shard, axis, pairs)  9.35 us
  transfers between devices with their start and end apart: 10, of which 6 were waited for; matrix products, arithmetic and copies ran while one was open for 0% of the time, Pallas kernels for 0%

commit v1 on v0

v1 whole, which is shorter than its diff:
```python
import functools

import jax
import jax.numpy as jnp
from jax import lax
from jax.experimental import pallas as pl
from jax.experimental.pallas import tpu as pltpu
from jax.sharding import PartitionSpec as P

NZ = 96
KMIN = 0.001
MESH = pl.DeviceIdType.MESH
LANES = 128
LOADS = 8
XC = 16
YC = 8
XN, YN = XC + 4, YC + 4
SIDES = [(dx, dy) for dx in (-1, 0, 1) for dy in (-1, 0, 1) if (dx, dy) != (0, 0)]

HEAT_FROM = {1: (XC, 2), 0: (2, XC), -1: (2, 2)}
HEAT_TO = {1: (0, 2), 0: (2, XC), -1: (XC + 2, 2)}
HEATY_FROM = {1: (YC, 2), 0: (2, YC), -1: (2, 2)}
HEATY_TO = {1: (0, 2), 0: (2, YC), -1: (YC + 2, 2)}
DENS_FROM = {1: (16, 8), 0: (8, 16), -1: (8, 8)}
DENS_TO = {1: (0, 8), 0: (8, 16), -1: (24, 8)}
DENSY_FROM = {1: (768, 384), 0: (384, 768), -1: (384, 256)}
DENSY_TO = {1: (0, 384), 0: (384, 768), -1: (1152, 256)}


TILES = YC * NZ // LANES
TILE_STEP = XC * TILES


def to_tiles(field):
    parts = field.reshape(LOADS, XC // 8, 8, TILES, LANES)
    return parts.transpose(0, 1, 3, 2, 4).reshape(LOADS * TILE_STEP, LANES)


def from_tiles(rows):
    parts = rows.reshape(LOADS, XC // 8, TILES, 8, LANES)
    return parts.transpose(0, 1, 3, 2, 4).reshape(LOADS, XC, TILES * LANES)


def tile_row(x, tile):
    return (x // 8) * (8 * TILES) + lax.rem(x, 8) + 8 * tile


def spread_lanes(tile_of, y, lane):
    first = (y * NZ) // LANES
    kind = y % 4
    if kind == 0:
        return tile_of(first)
    if kind == 1:
        return pltpu.roll(jnp.where(lane >= 96, tile_of(first), tile_of(first + 1)), 32, 1)
    if kind == 2:
        return pltpu.roll(jnp.where(lane >= 64, tile_of(first), tile_of(first + 1)), 64, 1)
    return pltpu.roll(tile_of(first), 96, 1)


def pack_lanes(cols, lane):
    one = pltpu.roll(cols[1], 96, 1)
    two = pltpu.roll(cols[2], 64, 1)
    three = pltpu.roll(cols[3], 32, 1)
    return (
        jnp.where(lane < 96, cols[0], one),
        jnp.where(lane < 64, one, two),
        jnp.where(lane < 32, two, three),
    )


def row_of(ref, col, row):
    return jnp.broadcast_to(ref[col, pl.ds(row, 1), :], (LOADS, LANES))


def element_row(low, high, coef):
    v0, w0 = low
    v1, w1 = high
    count = len(v0)
    b0l, b1l, t0l, t1l = [[None] * count for _ in range(4)]

    def add(acc, at, val):
        acc[at] = val if acc[at] is None else acc[at] + val

    for y in range(count - 1):
        even = (v0[y] + w0[y + 1]) + (w1[y] + v1[y + 1])
        odd = (w0[y] + v0[y + 1]) + (v1[y] + w1[y + 1])
        c = coef(y)
        add(b0l, y, c * (even + w1[y + 1]))
        add(b1l, y, c * (odd + v1[y + 1]))
        add(b0l, y + 1, c * (odd + w1[y]))
        add(b1l, y + 1, c * (even + v1[y]))
        add(t0l, y, c * (odd + w0[y + 1]))
        add(t1l, y, c * (even + v0[y + 1]))
        add(t0l, y + 1, c * (even + w0[y]))
        add(t1l, y + 1, c * (odd + v0[y]))
    return (b0l, b1l), (t0l, t1l)


def apply_rows(load_row, coef_at, rows, cols, emit, start):
    def both(i):
        v = load_row(i)
        return v, [pltpu.roll(t, LANES - 1, 1) for t in v]

    inner = range(1, cols - 1)
    low = both(0)
    high = both(1)
    _, top = element_row(low, high, lambda y: coef_at(0, y))

    def body(i, carry):
        v0, w0, t0, t1, extra = carry
        nxt = both(i + 1)
        (b0, b1), (n0, n1) = element_row((v0, w0), nxt, lambda y: coef_at(i, y))
        sums = {
            y: (t0[k] + b0[y]) + pltpu.roll(t1[k] + b1[y], 1, 1) for k, y in enumerate(inner)
        }
        extra = emit(i, sums, extra)
        return nxt[0], nxt[1], [n0[y] for y in inner], [n1[y] for y in inner], extra

    first = (high[0], high[1], [top[0][y] for y in inner], [top[1][y] for y in inner], start)
    return lax.fori_loop(1, rows - 1, body, first)[4]


def kernel(
    gxn, lown, hin, h_hbm, d_hbm, x_out, r_out,
    hv, dd, rv, zv, qv, yv, pv, cu, mi, rows, got0, got1, got2,
    in_sem, heat_send, heat_recv, dens_send, dens_recv, sum_send, sum_recv,
):
    gyn = lown * hin
    ix, iy = lax.axis_index("gx"), lax.axis_index("gy")
    lo, hi = lax.rem(iy, lown), iy // lown
    beside = [
        (lax.rem(ix + dx + gxn, gxn), lax.rem(iy + dy + gyn, gyn)) for dx, dy in SIDES
    ]
    groups = [
        [(ix, hi * lown + lax.rem(lo + r, lown)) for r in range(1, lown)],
        [(ix, lax.rem(hi + r, hin) * lown + lo) for r in range(1, hin)],
        [(lax.rem(ix + r, gxn), iy) for r in range(1, gxn)],
    ]
    partners = beside + groups[0] + groups[1] + groups[2]

    barrier = pltpu.get_barrier_semaphore()
    for one in partners:
        pl.semaphore_signal(barrier, inc=1, device_id=one, device_id_type=MESH)
    take_d = pltpu.make_async_copy(d_hbm, dd.at[pl.ds(8, 16), pl.ds(384, 768)], in_sem.at[1])
    take_h = pltpu.make_async_copy(h_hbm, hv, in_sem.at[0])
    take_h.start()
    take_d.start()
    lane = lax.broadcasted_iota(jnp.int32, (LOADS, LANES), 1)
    sub = lax.broadcasted_iota(jnp.int32, (LOADS, LANES), 0)
    live = lane < NZ
    take_h.wait()

    def lay_out(x, carry):
        tiles = [hv[pl.ds(tile_row(x, t), LOADS, stride=TILE_STEP), :] for t in range(6)]
        for y in range(YC):
            rv[x + 2, y + 2] = jnp.where(live, spread_lanes(lambda t: tiles[t], y, lane), 0.0)
        return carry

    lax.fori_loop(0, XC, lay_out, 0)
    take_d.wait()
    pl.semaphore_wait(barrier, len(partners))

    heat, dens = [], []
    for k, (dx, dy) in enumerate(SIDES):
        copy = pltpu.make_async_remote_copy(
            src_ref=dd.at[pl.ds(*DENS_FROM[dx]), pl.ds(*DENSY_FROM[dy])],
            dst_ref=dd.at[pl.ds(*DENS_TO[dx]), pl.ds(*DENSY_TO[dy])],
            send_sem=dens_send.at[k],
            recv_sem=dens_recv.at[k],
            device_id=beside[k],
            device_id_type=MESH,
        )
        copy.start()
        dens.append(copy)
    for k, (dx, dy) in enumerate(SIDES):
        copy = pltpu.make_async_remote_copy(
            src_ref=rv.at[pl.ds(*HEAT_FROM[dx]), pl.ds(*HEATY_FROM[dy])],
            dst_ref=rv.at[pl.ds(*HEAT_TO[dx]), pl.ds(*HEATY_TO[dy])],
            send_sem=heat_send.at[k],
            recv_sem=heat_recv.at[k],
            device_id=beside[k],
            device_id_type=MESH,
        )
        copy.start()
        heat.append(copy)

    for copy in dens:
        copy.wait_recv()
    for octet in range(4):
        x = sub + (8 * octet - 8)
        x_in = ((x >= 0) | (ix > 0)) & ((x < XC) | (ix < gxn - 1)) & live
        for ey in range(13):
            flat = spread_lanes(
                lambda t, octet=octet: dd[pl.ds(8 * octet, 8), pl.ds(LANES * t, LANES)], ey + 1, lane
            )
            y = ey - 3
            inside = x_in
            if y < 0:
                inside = inside & (iy > 0)
            if y >= YC:
                inside = inside & (iy < gyn - 1)
            c = KMIN + (1.0 - KMIN) * (flat * flat * flat)
            cu[ey, pl.ds(8 * octet, 8), :] = jnp.where(inside, c * (1.0 / 12.0), 0.0)
    lane32 = lax.broadcasted_iota(jnp.int32, (32, LANES), 1)
    x32 = lax.broadcasted_iota(jnp.int32, (32, LANES), 0) - 8
    x_in32 = ((x32 >= 0) | (ix > 0)) & ((x32 < XC) | (ix < gxn - 1)) & (lane32 < NZ)
    for ny in range(YN):
        both = cu[ny] + cu[ny + 1]
        both = both + pltpu.roll(both, 1, 1)
        both = 4.0 * (both + pltpu.roll(both, 1, 0))
        inside = x_in32
        if ny < 2:
            inside = inside & (iy > 0)
        if ny >= YC + 2:
            inside = inside & (iy < gyn - 1)
        mi[ny] = jnp.where(inside, 1.0 / both, 0.0)

    for copy in heat:
        copy.wait_recv()

    def scaled_row(i):
        out = []
        for y in range(YN):
            z = rv[i, y] * row_of(mi, y, i + 6)
            zv[i, y] = z
            out.append(z)
        return out

    def emit_image(i, sums, extra):
        for y, off in sums.items():
            q = 1.25 * rv[i, y] - off
            qv[i - 1, y - 1] = q
            yv[i - 1, y - 1] = q * row_of(mi, y, i + 6)
        return extra

    apply_rows(scaled_row, lambda i, y: row_of(cu, y + 1, i + 6), XN, YN, emit_image, 0)

    def emit_second(i, sums, extra):
        s0, s1, s2, s3 = extra
        for y, off in sums.items():
            q = qv[i, y]
            yy = yv[i, y]
            z = zv[i + 1, y + 1]
            p = 1.25 * q - off
            pv[i - 1, y - 1] = p
            s0 = s0 + rv[i + 1, y + 1] * z
            s1 = s1 + z * q
            s2 = s2 + yy * q
            s3 = s3 + yy * p
        return s0, s1, s2, s3

    zero = jnp.zeros((LOADS, LANES), jnp.float32)
    moments = apply_rows(
        lambda i: [yv[i, y] for y in range(YC + 2)],
        lambda i, y: row_of(cu, y + 2, i + 7),
        XC + 2,
        YC + 2,
        emit_second,
        (zero,) * 4,
    )

    spot = zero
    for k in range(4):
        total = jnp.sum(moments[k], axis=1, keepdims=True)
        spot = spot + jnp.where(lane == 4 * sub + k, total, 0.0)
    rows[0] = jnp.sum(spot, axis=0, keepdims=True)
    sent = []
    done = 0
    for step, (group, got) in enumerate(zip(groups, (got0, got1, got2))):
        copies = []
        for r, one in enumerate(group):
            copies.append(
                pltpu.make_async_remote_copy(
                    src_ref=rows.at[step],
                    dst_ref=got.at[r],
                    send_sem=sum_send.at[done + r],
                    recv_sem=sum_recv.at[done + r],
                    device_id=one,
                    device_id_type=MESH,
                )
            )
        half = len(copies) // 2
        for r in sorted(range(len(copies)), key=lambda r: abs(r - half)):
            copies[r].start()
        for copy in copies:
            copy.wait_recv()
        done += len(copies)
        sent += copies
        total = rows[step]
        for r in range(len(copies)):
            total = total + got[r]
        rows[step + 1] = total

    whole = jnp.broadcast_to(rows[3], (LOADS, LANES))
    s0, s1, s2, s3 = [
        jnp.sum(jnp.where(lane == 4 * sub + k, whole, 0.0), axis=1, keepdims=True) for k in range(4)
    ]
    a0 = s0 / s1
    g = s2 / s1
    mu = (a0 * g - 1.0) / (s3 / s1 - g * g)
    first = jnp.broadcast_to(a0 + mu * g, (LOADS, LANES))
    mu = jnp.broadcast_to(mu, (LOADS, LANES))

    def finish(x, carry):
        for part in range(2):
            xs, rs = [], []
            for k in range(4):
                y = 4 * part + k
                xs.append(first * zv[x + 2, y + 2] - mu * yv[x + 1, y + 1])
                rs.append(rv[x + 2, y + 2] - first * qv[x + 1, y + 1] + mu * pv[x, y])
            for out, cols in ((x_out, xs), (r_out, rs)):
                for t, tile in enumerate(pack_lanes(cols, lane)):
                    out[pl.ds(tile_row(x, 3 * part + t), LOADS, stride=TILE_STEP), :] = tile
        return carry

    lax.fori_loop(0, XC, finish, 0)
    for copy in dens + heat + sent:
        copy.wait_send()


def solution(mesh):
    gxn, gyn = mesh.shape["gx"], mesh.shape["gy"]
    lown = 8 if gyn % 8 == 0 and gyn > 8 else 2
    hin = gyn // lown
    count = (lown - 1) + (hin - 1) + (gxn - 1)

    def per_device(heat_source, density):
        loads, xc, flat = heat_source.shape
        out = jax.ShapeDtypeStruct((loads * xc * flat // LANES, LANES), jnp.float32)
        f32 = jnp.float32
        dma = pltpu.SemaphoreType.DMA
        sol, res = pl.pallas_call(
            functools.partial(kernel, gxn, lown, hin),
            out_shape=(out, out),
            in_specs=[pl.BlockSpec(memory_space=pltpu.HBM)] * 2,
            out_specs=[pl.BlockSpec(memory_space=pltpu.VMEM)] * 2,
            scratch_shapes=[
                pltpu.VMEM((loads * xc * flat // LANES, LANES), f32),
                pltpu.VMEM((32, 1408), f32),
                pltpu.VMEM((XN, YN, LOADS, LANES), f32),
                pltpu.VMEM((XN, YN, LOADS, LANES), f32),
                pltpu.VMEM((XC + 2, YC + 2, LOADS, LANES), f32),
                pltpu.VMEM((XC + 2, YC + 2, LOADS, LANES), f32),
                pltpu.VMEM((XC, YC, LOADS, LANES), f32),
                pltpu.VMEM((13, 32, LANES), f32),
                pltpu.VMEM((YN, 32, LANES), f32),
                pltpu.VMEM((4, 1, LANES), f32),
                pltpu.VMEM((lown - 1, 1, LANES), f32),
                pltpu.VMEM((hin - 1, 1, LANES), f32),
                pltpu.VMEM((gxn - 1, 1, LANES), f32),
                dma((2,)),
                dma((8,)),
                dma((8,)),
                dma((8,)),
                dma((8,)),
                dma((count,)),
                dma((count,)),
            ],
            compiler_params=pltpu.CompilerParams(
                collective_id=0, has_side_effects=True, vmem_limit_bytes=32 * 1024 * 1024
            ),
            name="two_steps",
        )(to_tiles(heat_source), density)
        return from_tiles(sol), from_tiles(res)

    placed = P(None, "gx", "gy")
    return jax.shard_map(
        per_device,
        mesh=mesh,
        in_specs=(placed, P("gx", "gy")),
        out_specs=(placed, placed),
        check_vma=False,
    )
```

time: 419 us -> 50.3 us (0.12); the launches traced: 414 us -> 50 us
  blocking collectives: 332 us -> 0 us
  Pallas kernels: 0 us -> 46.1 us
  starting transfers between devices: 31.8 us -> 0 us
  waiting for transfers between devices: 18.6 us -> 0 us
  other arithmetic: 12 us -> 0 us
  matrix products: 11.9 us -> 0 us
    psum x3 -> x0, blocking collectives: 332 us -> none  [the longest x2 224 us: residual_dot(): return lax.psum(local_sums(residual, scaled), ('gx', 'gy'))]
    pallas_call x0 -> x1, Pallas kernels: none -> 46.1 us  [per_device(): pl.pallas_call(functools.partial(kernel, gxn, lown, hin), out_shape=(out,...]
    ppermute x10 -> x0, starting transfers between devices: 31.8 us -> none  [the longest x4 15.1 us: with_halo(): lax.ppermute(lax.slice_in_dim(block, block.shape[dim] - width, None, axis...]
    ppermute x10 -> x0, waiting for transfers between devices: 18.6 us -> none  [the longest x4 13.1 us: with_halo(): lax.ppermute(lax.slice_in_dim(block, 0, width, axis=dim), axis, backward)]
    dot_general x2 -> x0, matrix products: 11.9 us -> none  [block_apply(): jnp.einsum('nm,mlag->nlag', k_elem, corner_vals, precision=lax.Precision....]
    add x4 -> x0, other arithmetic: 6.25 us -> none  [the longest x2 5.33 us: spread_nodes(): summed = piece if summed is None else summed + piece]
  transfers between devices with their start and end apart: 10 -> 0, of which waited for: 6 -> 0; matrix products, arithmetic and copies ran while one was open for 0% -> 0% of each run, Pallas kernels for 0% -> 0%
where the time goes in v1:
time: 50.3 us; the launch traced here: 50 us
  Pallas kernels  46.1 us (92%)
  local copies, waits for them, and re-layouts  3.28 us (7%)
  between operations  0.65 us (1%)
    pallas_call x1, Pallas kernels, per_device(): pl.pallas_call(functools.partial(kernel, gxn, lown, hin), out_shape=(out,...  46.1 us
    unnamed x6, local copies, waits for them, and re-layouts  3.28 us

profile of v1, /device:TPU:1, one launch (start us, length us, event | category | flops | bytes accessed | tf_op | source)
XLA Modules:
  0.0 50.0 jit_solution(5905312114606134588)
XLA Ops:
  0.6 0.0 copy-start
  0.6 1.0 %copy-done = f32[8,16,768]{2,1,0:T(8,128)S(1)} copy-done((f32[8,16,768]{2,1,0:T(8,128)S(1)}, f32[8,16,768]{2,1,0:T(8,128)}, u32[]{:S(2)}) %copy-start) | copy-done | bytes 393240
  1.6 0.0 copy-start.1
  1.6 0.8 %copy-done.1 = f32[16,768]{1,0:T(8,128)S(1)} copy-done((f32[16,768]{1,0:T(8,128)S(1)}, f32[16,768]{1,0:T(8,128)}, u32[]{:S(2)}) %copy-start.1) | copy-done | bytes 49176
  2.4 46.1 %two_steps.1 = (f32[768,128]{1,0:T(8,128)S(1)}, f32[768,128]{1,0:T(8,128)S(1)}) custom-call(f32[768,128]{1,0:T(8,128)S(1)} %bitcast.15, f32[16,768]{1,0:T(8,128)S(1)} %copy-done.1), custom_call_target="tpu_custom_call" | custom-call | tf_op jit(solution)/shard_map/two_steps/pallas_call | solution.py:332
  48.5 0.7 %copy.6 = f32[8,16,768]{2,1,0:T(8,128)} copy(f32[8,16,768]{2,1,0:T(8,128)S(1)} %bitcast.17) | data formatting | bytes 786432
  49.3 0.7 %copy.7 = f32[8,16,768]{2,1,0:T(8,128)} copy(f32[8,16,768]{2,1,0:T(8,128)S(1)} %bitcast.16) | data formatting | bytes 786432
Async XLA Ops:
  0.6 1.0 %copy-start = (f32[8,16,768]{2,1,0:T(8,128)S(1)}, f32[8,16,768]{2,1,0:T(8,128)}, u32[]{:S(2)}) copy-start(f32[8,16,768]{2,1,0:T(8,128)} %param.2) | copy-start | bytes 1179652
  1.6 0.8 %copy-start.1 = (f32[16,768]{1,0:T(8,128)S(1)}, f32[16,768]{1,0:T(8,128)}, u32[]{:S(2)}) copy-start(f32[16,768]{1,0:T(8,128)} %d_hbm.1) | copy-start | bytes 147460

commit v2 on v1

--- a/solution.py
+++ b/solution.py
@@ -11,6 +11,7 @@
 KMIN = 0.001
 MESH = pl.DeviceIdType.MESH
 LANES = 128
+GRANT = 53 * 1024 * 1024
 LOADS = 8
 XC = 16
 YC = 8
@@ -72,75 +73,110 @@
     return jnp.broadcast_to(ref[col, pl.ds(row, 1), :], (LOADS, LANES))
 
 
+def row_fields(tiles):
+    ups = [pltpu.roll(t, LANES - 1, 1) for t in tiles]
+    s = [t + u for t, u in zip(tiles, ups)]
+    d = [t - u for t, u in zip(tiles, ups)]
+    return s, d, [s[y] + s[y + 1] for y in range(len(s) - 1)]
+
+
 def element_row(low, high, coef):
-    v0, w0 = low
-    v1, w1 = high
-    count = len(v0)
-    b0l, b1l, t0l, t1l = [[None] * count for _ in range(4)]
-
-    def add(acc, at, val):
-        acc[at] = val if acc[at] is None else acc[at] + val
-
-    for y in range(count - 1):
-        even = (v0[y] + w0[y + 1]) + (w1[y] + v1[y + 1])
-        odd = (w0[y] + v0[y + 1]) + (v1[y] + w1[y + 1])
+    s0, d0, p0 = low
+    s1, d1, p1 = high
+    ct, c1, c2, cq, cp = [[] for _ in range(5)]
+    for y in range(len(s0) - 1):
         c = coef(y)
-        add(b0l, y, c * (even + w1[y + 1]))
-        add(b1l, y, c * (odd + v1[y + 1]))
-        add(b0l, y + 1, c * (odd + w1[y]))
-        add(b1l, y + 1, c * (even + v1[y]))
-        add(t0l, y, c * (odd + w0[y + 1]))
-        add(t1l, y, c * (even + v0[y + 1]))
-        add(t0l, y + 1, c * (even + w0[y]))
-        add(t1l, y + 1, c * (odd + v0[y]))
-    return (b0l, b1l), (t0l, t1l)
-
-
-def apply_rows(load_row, coef_at, rows, cols, emit, start):
-    def both(i):
-        v = load_row(i)
-        return v, [pltpu.roll(t, LANES - 1, 1) for t in v]
-
-    inner = range(1, cols - 1)
-    low = both(0)
-    high = both(1)
-    _, top = element_row(low, high, lambda y: coef_at(0, y))
+        ct.append(c * (p0[y] + p1[y]))
+        c1.append(c * (s0[y] - s1[y + 1]))
+        c2.append(c * (s0[y + 1] - s1[y]))
+        cq.append(c * (d0[y + 1] + d1[y]))
+        cp.append(c * (d0[y] + d1[y + 1]))
+    inner = range(1, len(s0) - 1)
+    u = [ct[y] + ct[y - 1] for y in inner]
+    below = (
+        [(c1[y] + c2[y - 1]) - u[y - 1] for y in inner],
+        [cq[y] + cp[y - 1] for y in inner],
+    )
+    above = (
+        [(c1[y - 1] + c2[y]) + u[y - 1] for y in inner],
+        [cq[y - 1] + cp[y] for y in inner],
+    )
+    return below, above
+
+
+def apply_rows(load_row, coef_at, rows, emit, start):
+    first_row = row_fields(load_row(0))
+    second = row_fields(load_row(1))
+    _, above = element_row(first_row, second, lambda y: coef_at(0, y))
 
     def body(i, carry):
-        v0, w0, t0, t1, extra = carry
-        nxt = both(i + 1)
-        (b0, b1), (n0, n1) = element_row((v0, w0), nxt, lambda y: coef_at(i, y))
-        sums = {
-            y: (t0[k] + b0[y]) + pltpu.roll(t1[k] + b1[y], 1, 1) for k, y in enumerate(inner)
-        }
-        extra = emit(i, sums, extra)
-        return nxt[0], nxt[1], [n0[y] for y in inner], [n1[y] for y in inner], extra
-
-    first = (high[0], high[1], [top[0][y] for y in inner], [top[1][y] for y in inner], start)
-    return lax.fori_loop(1, rows - 1, body, first)[4]
+        low, (tops, topd), extra = carry
+        high = row_fields(load_row(i + 1))
+        (bots, botd), above = element_row(low, high, lambda y: coef_at(i, y))
+        sums = []
+        for k in range(len(bots)):
+            n_s = bots[k] - tops[k]
+            n_d = botd[k] + topd[k]
+            sums.append((n_s + n_d) + pltpu.roll(n_s - n_d, 1, 1))
+        return high, above, emit(i, sums, extra)
+
+    return lax.fori_loop(1, rows - 1, body, (second, above, start))[2]
+
+
+def wrap(i, n):
+    return jnp.where(i >= n, i - n, i)
+
+
+def hops(n):
+    known, out = 1, []
+    while known < n // 2:
+        step = min(known, n // 2 - known)
+        out.append(step)
+        known += step
+    return out
 
 
 def kernel(
     gxn, lown, hin, h_hbm, d_hbm, x_out, r_out,
-    hv, dd, rv, zv, qv, yv, pv, cu, mi, rows, got0, got1, got2,
-    in_sem, heat_send, heat_recv, dens_send, dens_recv, sum_send, sum_recv,
+    hv, dd, rv, zv, qv, yv, pv, zp, yp, qp, pp, cu, mi, rows, got0, got1, got2,
+    in_sem, heat_send, heat_recv, dens_send, dens_recv, sum_send, sum_recv, known,
 ):
     gyn = lown * hin
     ix, iy = lax.axis_index("gx"), lax.axis_index("gy")
-    lo, hi = lax.rem(iy, lown), iy // lown
-    beside = [
-        (lax.rem(ix + dx + gxn, gxn), lax.rem(iy + dy + gyn, gyn)) for dx, dy in SIDES
+    hi = iy // lown
+    lo = iy - hi * lown
+    xs_at = {d: wrap(ix + (d + gxn if d < 0 else d), gxn) for d in (-1, 0, 1)}
+    ys_at = {d: wrap(iy + (d + gyn if d < 0 else d), gyn) for d in (-1, 0, 1)}
+    xs_at[0], ys_at[0] = ix, iy
+    beside = [(xs_at[dx], ys_at[dy]) for dx, dy in SIDES]
+    groups = [
+        [(ix, hi * lown + wrap(lo + r, lown)) for r in range(1, lown)],
+        [(ix, wrap(hi + r, hin) * lown + lo) for r in range(1, hin)],
+        [(wrap(ix + r, gxn), iy) for r in range(1, gxn)],
     ]
-    groups = [
-        [(ix, hi * lown + lax.rem(lo + r, lown)) for r in range(1, lown)],
-        [(ix, lax.rem(hi + r, hin) * lown + lo) for r in range(1, hin)],
-        [(lax.rem(ix + r, gxn), iy) for r in range(1, gxn)],
-    ]
-    partners = beside + groups[0] + groups[1] + groups[2]
+    near = beside + groups[0] + [groups[1][0], groups[1][-1]]
 
     barrier = pltpu.get_barrier_semaphore()
-    for one in partners:
+    for one in near:
         pl.semaphore_signal(barrier, inc=1, device_id=one, device_id_type=MESH)
+    turns = []
+    for ring, n in ((groups[1], hin), (groups[2], gxn)):
+        turns.append([(ring[d - 1], ring[n - 1 - d]) for d in hops(n)])
+    count = max(len(t) for t in turns)
+    turns = [[t[k] for t in turns if k < len(t)] for k in range(count)]
+    flat_turns = [(k, pair) for k, pairs in enumerate(turns) for pair in pairs]
+
+    def tell(k):
+        for at, (turn, pair) in enumerate(flat_turns):
+            if turn == k:
+                for one in pair:
+                    pl.semaphore_signal(known.at[at], inc=1, device_id=one, device_id_type=MESH)
+
+    def hear(k):
+        for at, (turn, _) in enumerate(flat_turns):
+            if turn == k:
+                pl.semaphore_wait(known.at[at], 2)
+
     take_d = pltpu.make_async_copy(d_hbm, dd.at[pl.ds(8, 16), pl.ds(384, 768)], in_sem.at[1])
     take_h = pltpu.make_async_copy(h_hbm, hv, in_sem.at[0])
     take_h.start()
@@ -158,7 +194,7 @@
 
     lax.fori_loop(0, XC, lay_out, 0)
     take_d.wait()
-    pl.semaphore_wait(barrier, len(partners))
+    pl.semaphore_wait(barrier, len(near))
 
     heat, dens = [], []
     for k, (dx, dy) in enumerate(SIDES):
@@ -184,8 +220,14 @@
         copy.start()
         heat.append(copy)
 
+    tell(0)
+
     for copy in dens:
         copy.wait_recv()
+    for k in range(1, count):
+        if k == 1:
+            hear(0)
+            tell(1)
     for octet in range(4):
         x = sub + (8 * octet - 8)
         x_in = ((x >= 0) | (ix > 0)) & ((x < XC) | (ix < gxn - 1)) & live
@@ -200,14 +242,14 @@
             if y >= YC:
                 inside = inside & (iy < gyn - 1)
             c = KMIN + (1.0 - KMIN) * (flat * flat * flat)
-            cu[ey, pl.ds(8 * octet, 8), :] = jnp.where(inside, c * (1.0 / 12.0), 0.0)
+            cu[ey, pl.ds(8 * octet, 8), :] = jnp.where(inside, c * (1.0 / 24.0), 0.0)
     lane32 = lax.broadcasted_iota(jnp.int32, (32, LANES), 1)
     x32 = lax.broadcasted_iota(jnp.int32, (32, LANES), 0) - 8
     x_in32 = ((x32 >= 0) | (ix > 0)) & ((x32 < XC) | (ix < gxn - 1)) & (lane32 < NZ)
     for ny in range(YN):
         both = cu[ny] + cu[ny + 1]
         both = both + pltpu.roll(both, 1, 1)
-        both = 4.0 * (both + pltpu.roll(both, 1, 0))
+        both = 8.0 * (both + pltpu.roll(both, 1, 0))
         inside = x_in32
         if ny < 2:
             inside = inside & (iy > 0)
@@ -215,8 +257,20 @@
             inside = inside & (iy < gyn - 1)
         mi[ny] = jnp.where(inside, 1.0 / both, 0.0)
 
+    zero = jnp.zeros((LOADS, LANES), jnp.float32)
+
+    def first_moment(x, s0):
+        for y in range(YC):
+            r = rv[x + 2, y + 2]
+            s0 = s0 + r * (r * row_of(mi, y + 2, x + 8))
+        return s0
+
+    s0 = lax.fori_loop(0, XC, first_moment, zero)
     for copy in heat:
         copy.wait_recv()
+    for k in range(1, count - 1):
+        hear(k)
+        tell(k + 1)
 
     def scaled_row(i):
         out = []
@@ -227,43 +281,49 @@
         return out
 
     def emit_image(i, sums, extra):
-        for y, off in sums.items():
-            q = 1.25 * rv[i, y] - off
-            qv[i - 1, y - 1] = q
-            yv[i - 1, y - 1] = q * row_of(mi, y, i + 6)
+        for y, off in enumerate(sums):
+            q = rv[i, y + 1] + off
+            qv[i - 1, y] = q
+            yv[i - 1, y] = q * row_of(mi, y + 1, i + 6)
         return extra
 
-    apply_rows(scaled_row, lambda i, y: row_of(cu, y + 1, i + 6), XN, YN, emit_image, 0)
+    apply_rows(scaled_row, lambda i, y: row_of(cu, y + 1, i + 6), XN, emit_image, 0)
 
     def emit_second(i, sums, extra):
-        s0, s1, s2, s3 = extra
-        for y, off in sums.items():
-            q = qv[i, y]
-            yy = yv[i, y]
-            z = zv[i + 1, y + 1]
-            p = 1.25 * q - off
-            pv[i - 1, y - 1] = p
-            s0 = s0 + rv[i + 1, y + 1] * z
-            s1 = s1 + z * q
+        s1, s2, s3 = extra
+        for y, off in enumerate(sums):
+            q = qv[i, y + 1]
+            yy = yv[i, y + 1]
+            p = q + off
+            pv[i - 1, y] = p
+            s1 = s1 + zv[i + 1, y + 2] * q
             s2 = s2 + yy * q
             s3 = s3 + yy * p
-        return s0, s1, s2, s3
-
-    zero = jnp.zeros((LOADS, LANES), jnp.float32)
+        return s1, s2, s3
+
     moments = apply_rows(
         lambda i: [yv[i, y] for y in range(YC + 2)],
         lambda i, y: row_of(cu, y + 2, i + 7),
         XC + 2,
-        YC + 2,
         emit_second,
-        (zero,) * 4,
+        (zero,) * 3,
     )
+    moments = (s0,) + tuple(moments)
+    hear(count - 1)
 
     spot = zero
     for k in range(4):
         total = jnp.sum(moments[k], axis=1, keepdims=True)
         spot = spot + jnp.where(lane == 4 * sub + k, total, 0.0)
     rows[0] = jnp.sum(spot, axis=0, keepdims=True)
+    def pack(x, carry):
+        for ref, out, dx, dy in ((zv, zp, 2, 2), (yv, yp, 1, 1), (qv, qp, 1, 1), (pv, pp, 0, 0)):
+            for part in range(2):
+                cols = [ref[x + dx, 4 * part + k + dy] for k in range(4)]
+                for t, tile in enumerate(pack_lanes(cols, lane)):
+                    out[pl.ds(tile_row(x, 3 * part + t), LOADS, stride=TILE_STEP), :] = tile
+        return carry
+
     sent = []
     done = 0
     for step, (group, got) in enumerate(zip(groups, (got0, got1, got2))):
@@ -282,6 +342,8 @@
         half = len(copies) // 2
         for r in sorted(range(len(copies)), key=lambda r: abs(r - half)):
             copies[r].start()
+        if step == len(groups) - 1:
+            lax.fori_loop(0, XC, pack, 0)
         for copy in copies:
             copy.wait_recv()
         done += len(copies)
@@ -298,24 +360,24 @@
     a0 = s0 / s1
     g = s2 / s1
     mu = (a0 * g - 1.0) / (s3 / s1 - g * g)
-    first = jnp.broadcast_to(a0 + mu * g, (LOADS, LANES))
-    mu = jnp.broadcast_to(mu, (LOADS, LANES))
-
-    def finish(x, carry):
-        for part in range(2):
-            xs, rs = [], []
-            for k in range(4):
-                y = 4 * part + k
-                xs.append(first * zv[x + 2, y + 2] - mu * yv[x + 1, y + 1])
-                rs.append(rv[x + 2, y + 2] - first * qv[x + 1, y + 1] + mu * pv[x, y])
-            for out, cols in ((x_out, xs), (r_out, rs)):
-                for t, tile in enumerate(pack_lanes(cols, lane)):
-                    out[pl.ds(tile_row(x, 3 * part + t), LOADS, stride=TILE_STEP), :] = tile
-        return carry
-
-    lax.fori_loop(0, XC, finish, 0)
+    first = a0 + mu * g
+    for load in range(LOADS):
+        f = jnp.broadcast_to(first[load : load + 1], (LOADS, LANES))
+        m = jnp.broadcast_to(mu[load : load + 1], (LOADS, LANES))
+        for t in range(TILE_STEP // 8):
+            at = pl.ds(load * TILE_STEP + 8 * t, 8)
+            x_out[at, :] = f * zp[at, :] - m * yp[at, :]
+            r_out[at, :] = (hv[at, :] - f * qp[at, :]) + m * pp[at, :]
     for copy in dens + heat + sent:
         copy.wait_send()
+
+
+def put_out(x, r, x_out, r_out, sem):
+    copies = [pltpu.make_async_copy(x, x_out, sem.at[0]), pltpu.make_async_copy(r, r_out, sem.at[1])]
+    for copy in copies:
+        copy.start()
+    for copy in copies:
+        copy.wait()
 
 
 def solution(mesh):
@@ -335,13 +397,17 @@
             in_specs=[pl.BlockSpec(memory_space=pltpu.HBM)] * 2,
             out_specs=[pl.BlockSpec(memory_space=pltpu.VMEM)] * 2,
             scratch_shapes=[
-                pltpu.VMEM((loads * xc * flat // LANES, LANES), f32),
+                pltpu.VMEM((LOADS * TILE_STEP, LANES), f32),
                 pltpu.VMEM((32, 1408), f32),
                 pltpu.VMEM((XN, YN, LOADS, LANES), f32),
                 pltpu.VMEM((XN, YN, LOADS, LANES), f32),
                 pltpu.VMEM((XC + 2, YC + 2, LOADS, LANES), f32),
                 pltpu.VMEM((XC + 2, YC + 2, LOADS, LANES), f32),
                 pltpu.VMEM((XC, YC, LOADS, LANES), f32),
+                pltpu.VMEM((LOADS * TILE_STEP, LANES), f32),
+                pltpu.VMEM((LOADS * TILE_STEP, LANES), f32),
+                pltpu.VMEM((LOADS * TILE_STEP, LANES), f32),
+                pltpu.VMEM((LOADS * TILE_STEP, LANES), f32),
                 pltpu.VMEM((13, 32, LANES), f32),
                 pltpu.VMEM((YN, 32, LANES), f32),
                 pltpu.VMEM((4, 1, LANES), f32),
@@ -355,12 +421,22 @@
                 dma((8,)),
                 dma((count,)),
                 dma((count,)),
+                pltpu.SemaphoreType.REGULAR((len(hops(hin)) + len(hops(gxn)),)),
             ],
             compiler_params=pltpu.CompilerParams(
-                collective_id=0, has_side_effects=True, vmem_limit_bytes=32 * 1024 * 1024
+                collective_id=0, has_side_effects=True, vmem_limit_bytes=GRANT
             ),
             name="two_steps",
         )(to_tiles(heat_source), density)
+        sol, res = pl.pallas_call(
+            put_out,
+            out_shape=(out, out),
+            in_specs=[pl.BlockSpec(memory_space=pltpu.VMEM)] * 2,
+            out_specs=[pl.BlockSpec(memory_space=pltpu.HBM)] * 2,
+            scratch_shapes=[dma((2,))],
+            compiler_params=pltpu.CompilerParams(vmem_limit_bytes=2 * 1024 * 1024),
+            name="put_out",
+        )(sol, res)
         return from_tiles(sol), from_tiles(res)
 
     placed = P(None, "gx", "gy")

time: 50.3 us -> 47.5 us (0.944)
  the two profiles are of different devices: /device:TPU:1 before, /device:TPU:2 now
where the time goes in v2:
time: 47.5 us; the launch traced here: 47.3 us
  Pallas kernels  45.8 us (96%)
  local copies, waits for them, and re-layouts  0.79 us (2%)
  between operations  0.65 us (1%)
    pallas_call x1, Pallas kernels, per_device(): pl.pallas_call(functools.partial(kernel, gxn, lown, hin), out_shape=(out,...  44.9 us

profile of v2, /device:TPU:2, one launch (start us, length us, event | category | flops | bytes accessed | tf_op | source)
XLA Modules:
  0.0 47.3 jit_solution(12960124654800162653)
XLA Ops:
  0.6 0.0 copy-start
  0.6 0.8 %copy-done = f32[16,768]{1,0:T(8,128)S(1)} copy-done((f32[16,768]{1,0:T(8,128)S(1)}, f32[16,768]{1,0:T(8,128)}, u32[]{:S(2)}) %copy-start) | copy-done | bytes 49176
  1.4 44.9 %two_steps.1 = (f32[768,128]{1,0:T(8,128)S(1)}, f32[768,128]{1,0:T(8,128)S(1)}) custom-call(f32[768,128]{1,0:T(8,128)} %bitcast.15, f32[16,768]{1,0:T(8,128)S(1)} %copy-done), custom_call_target="tpu_custom_call" | custom-call | tf_op jit(solution)/shard_map/two_steps/pallas_call | solution.py:394
  46.4 0.9 %put_out.1 = (f32[768,128]{1,0:T(8,128)}, f32[768,128]{1,0:T(8,128)}) custom-call(f32[768,128]{1,0:T(8,128)S(1)} %get-tuple-element.6.x, f32[768,128]{1,0:T(8,128)S(1)} %get-tuple-element.7.r), custom_call_target="tpu_custom_call" | custom-call | tf_op jit(solution)/shard_map/put_out/pallas_call | solution.py:431
Async XLA Ops:
  0.6 0.8 %copy-start = (f32[16,768]{1,0:T(8,128)S(1)}, f32[16,768]{1,0:T(8,128)}, u32[]{:S(2)}) copy-start(f32[16,768]{1,0:T(8,128)} %d_hbm.1) | copy-start | bytes 147460

commit v3 on v2

--- a/solution.py
+++ b/solution.py
@@ -1,4 +1,5 @@
 import functools
+import math
 
 import jax
 import jax.numpy as jnp
@@ -12,6 +13,7 @@
 MESH = pl.DeviceIdType.MESH
 LANES = 128
 GRANT = 53 * 1024 * 1024
+BY_IMAGE, BY_SECOND = 6, 8
 LOADS = 8
 XC = 16
 YC = 8
@@ -104,7 +106,7 @@
     return below, above
 
 
-def apply_rows(load_row, coef_at, rows, emit, start):
+def apply_rows(load_row, coef_at, rows, emit, start, by):
     first_row = row_fields(load_row(0))
     second = row_fields(load_row(1))
     _, above = element_row(first_row, second, lambda y: coef_at(0, y))
@@ -120,25 +122,43 @@
             sums.append((n_s + n_d) + pltpu.roll(n_s - n_d, 1, 1))
         return high, above, emit(i, sums, extra)
 
-    return lax.fori_loop(1, rows - 1, body, (second, above, start))[2]
+    return walk(1, rows - 1, body, (second, above, start), by)[2]
+
+
+def walk(start, stop, body, carry, by):
+    def turn(t, carry):
+        for k in range(by):
+            carry = body(start + t * by + k, carry)
+        return carry
+
+    turns = (stop - start) // by
+    if turns == 1:
+        for k in range(by):
+            carry = body(start + k, carry)
+        return carry
+    return lax.fori_loop(0, turns, turn, carry)
 
 
 def wrap(i, n):
     return jnp.where(i >= n, i - n, i)
 
 
-def hops(n):
-    known, out = 1, []
+def hops(n, known):
+    ahead, out = 1 - known, []
     while known < n // 2:
-        step = min(known, n // 2 - known)
+        step = min(known + ahead, n // 2 - known)
         out.append(step)
         known += step
     return out
 
 
+def turns_of(xn, yn, zn):
+    return [(1, 1, zn, 2), (xn, yn, 1, 1)]
+
+
 def kernel(
     gxn, lown, hin, h_hbm, d_hbm, x_out, r_out,
-    hv, dd, rv, zv, qv, yv, pv, zp, yp, qp, pp, cu, mi, rows, got0, got1, got2,
+    hv, dd, rv, zv, qv, yv, pv, zp, yp, qp, pp, cu, mi, rows, got,
     in_sem, heat_send, heat_recv, dens_send, dens_recv, sum_send, sum_recv, known,
 ):
     gyn = lown * hin
@@ -149,19 +169,35 @@
     ys_at = {d: wrap(iy + (d + gyn if d < 0 else d), gyn) for d in (-1, 0, 1)}
     xs_at[0], ys_at[0] = ix, iy
     beside = [(xs_at[dx], ys_at[dy]) for dx, dy in SIDES]
-    groups = [
+    rings = [
         [(ix, hi * lown + wrap(lo + r, lown)) for r in range(1, lown)],
         [(ix, wrap(hi + r, hin) * lown + lo) for r in range(1, hin)],
         [(wrap(ix + r, gxn), iy) for r in range(1, gxn)],
     ]
-    near = beside + groups[0] + [groups[1][0], groups[1][-1]]
+    core = lo - 2 * (lo // 2)
+    groups = []
+    for xs, ys, zs, cores in turns_of(lown // 2, hin, gxn):
+        group = []
+        for dx in range(xs):
+            for dy in range(ys):
+                for dz in range(zs):
+                    for dc in range(cores):
+                        far = sum(min(d, n - d) for d, n in ((dx, xs), (dy, ys), (dz, zs)))
+                        if far + dc == 0:
+                            continue
+                        at = wrap(lo + 2 * dx, lown)
+                        if dc:
+                            at = at + 1 - 2 * core
+                        group.append((-far, (wrap(ix + dz, gxn), wrap(hi + dy, hin) * lown + at)))
+        groups.append([one for _, one in sorted(group, key=lambda g: g[0])])
+    near = beside + rings[0] + [rings[1][0], rings[1][-1]]
 
     barrier = pltpu.get_barrier_semaphore()
     for one in near:
         pl.semaphore_signal(barrier, inc=1, device_id=one, device_id_type=MESH)
     turns = []
-    for ring, n in ((groups[1], hin), (groups[2], gxn)):
-        turns.append([(ring[d - 1], ring[n - 1 - d]) for d in hops(n)])
+    for ring, n, known_at in ((rings[1], hin, 0), (rings[2], gxn, 1)):
+        turns.append([(ring[d - 1], ring[n - 1 - d]) for d in hops(n, known_at)])
     count = max(len(t) for t in turns)
     turns = [[t[k] for t in turns if k < len(t)] for k in range(count)]
     flat_turns = [(k, pair) for k, pairs in enumerate(turns) for pair in pairs]
@@ -192,7 +228,7 @@
             rv[x + 2, y + 2] = jnp.where(live, spread_lanes(lambda t: tiles[t], y, lane), 0.0)
         return carry
 
-    lax.fori_loop(0, XC, lay_out, 0)
+    walk(0, XC, lay_out, 0, 4)
     take_d.wait()
     pl.semaphore_wait(barrier, len(near))
 
@@ -265,7 +301,7 @@
             s0 = s0 + r * (r * row_of(mi, y + 2, x + 8))
         return s0
 
-    s0 = lax.fori_loop(0, XC, first_moment, zero)
+    s0 = walk(0, XC, first_moment, zero, 2)
     for copy in heat:
         copy.wait_recv()
     for k in range(1, count - 1):
@@ -287,7 +323,7 @@
             yv[i - 1, y] = q * row_of(mi, y + 1, i + 6)
         return extra
 
-    apply_rows(scaled_row, lambda i, y: row_of(cu, y + 1, i + 6), XN, emit_image, 0)
+    apply_rows(scaled_row, lambda i, y: row_of(cu, y + 1, i + 6), XN, emit_image, 0, BY_IMAGE)
 
     def emit_second(i, sums, extra):
         s1, s2, s3 = extra
@@ -307,6 +343,7 @@
         XC + 2,
         emit_second,
         (zero,) * 3,
+        BY_SECOND,
     )
     moments = (s0,) + tuple(moments)
     hear(count - 1)
@@ -326,34 +363,33 @@
 
     sent = []
     done = 0
-    for step, (group, got) in enumerate(zip(groups, (got0, got1, got2))):
+    for step, group in enumerate(groups):
         copies = []
         for r, one in enumerate(group):
             copies.append(
                 pltpu.make_async_remote_copy(
                     src_ref=rows.at[step],
-                    dst_ref=got.at[r],
+                    dst_ref=got.at[done + r],
                     send_sem=sum_send.at[done + r],
                     recv_sem=sum_recv.at[done + r],
                     device_id=one,
                     device_id_type=MESH,
                 )
             )
-        half = len(copies) // 2
-        for r in sorted(range(len(copies)), key=lambda r: abs(r - half)):
-            copies[r].start()
+        for copy in copies:
+            copy.start()
         if step == len(groups) - 1:
-            lax.fori_loop(0, XC, pack, 0)
+            walk(0, XC, pack, 0, 2)
         for copy in copies:
             copy.wait_recv()
+        total = rows[step]
+        for r in range(len(copies)):
+            total = total + got[done + r]
+        rows[step + 1] = total
         done += len(copies)
         sent += copies
-        total = rows[step]
-        for r in range(len(copies)):
-            total = total + got[r]
-        rows[step + 1] = total
-
-    whole = jnp.broadcast_to(rows[3], (LOADS, LANES))
+
+    whole = jnp.broadcast_to(rows[len(groups)], (LOADS, LANES))
     s0, s1, s2, s3 = [
         jnp.sum(jnp.where(lane == 4 * sub + k, whole, 0.0), axis=1, keepdims=True) for k in range(4)
     ]
@@ -384,7 +420,7 @@
     gxn, gyn = mesh.shape["gx"], mesh.shape["gy"]
     lown = 8 if gyn % 8 == 0 and gyn > 8 else 2
     hin = gyn // lown
-    count = (lown - 1) + (hin - 1) + (gxn - 1)
+    count = sum(math.prod(t) - 1 for t in turns_of(lown // 2, hin, gxn))
 
     def per_device(heat_source, density):
         loads, xc, flat = heat_source.shape
@@ -411,9 +447,7 @@
                 pltpu.VMEM((13, 32, LANES), f32),
                 pltpu.VMEM((YN, 32, LANES), f32),
                 pltpu.VMEM((4, 1, LANES), f32),
-                pltpu.VMEM((lown - 1, 1, LANES), f32),
-                pltpu.VMEM((hin - 1, 1, LANES), f32),
-                pltpu.VMEM((gxn - 1, 1, LANES), f32),
+                pltpu.VMEM((count, 1, LANES), f32),
                 dma((2,)),
                 dma((8,)),
                 dma((8,)),
@@ -421,7 +455,7 @@
                 dma((8,)),
                 dma((count,)),
                 dma((count,)),
-                pltpu.SemaphoreType.REGULAR((len(hops(hin)) + len(hops(gxn)),)),
+                pltpu.SemaphoreType.REGULAR((len(hops(hin, 0)) + len(hops(gxn, 1)),)),
             ],
             compiler_params=pltpu.CompilerParams(
                 collective_id=0, has_side_effects=True, vmem_limit_bytes=GRANT

time: 47.5 us -> 42 us (0.88)
  the two profiles are of different devices: /device:TPU:2 before, /device:TPU:1 now
where the time goes in v3:
time: 42 us; the launch traced here: 41.7 us
  Pallas kernels  40.3 us (96%)
  local copies, waits for them, and re-layouts  0.79 us (2%)
  between operations  0.65 us (2%)
    pallas_call x1, Pallas kernels, per_device(): pl.pallas_call(functools.partial(kernel, gxn, lown, hin), out_shape=(out,...  39.4 us
    pallas_call x1, Pallas kernels, per_device(): pl.pallas_call(put_out, out_shape=(out, out), in_specs=[pl.BlockSpec(memo...  0.89 us

profile of v3, /device:TPU:1, one launch (start us, length us, event | category | flops | bytes accessed | tf_op | source)
XLA Modules:
  0.0 41.7 jit_solution(3218052815285800430)
XLA Ops:
  0.6 0.0 copy-start
  0.6 0.8 %copy-done = f32[16,768]{1,0:T(8,128)S(1)} copy-done((f32[16,768]{1,0:T(8,128)S(1)}, f32[16,768]{1,0:T(8,128)}, u32[]{:S(2)}) %copy-start) | copy-done | bytes 49176
  1.4 39.4 %two_steps.1 = (f32[768,128]{1,0:T(8,128)S(1)}, f32[768,128]{1,0:T(8,128)S(1)}) custom-call(f32[768,128]{1,0:T(8,128)} %bitcast.15, f32[16,768]{1,0:T(8,128)S(1)} %copy-done), custom_call_target="tpu_custom_call" | custom-call | tf_op jit(solution)/shard_map/two_steps/pallas_call | solution.py:430
  40.8 0.9 %put_out.1 = (f32[768,128]{1,0:T(8,128)}, f32[768,128]{1,0:T(8,128)}) custom-call(f32[768,128]{1,0:T(8,128)S(1)} %get-tuple-element.6.x, f32[768,128]{1,0:T(8,128)S(1)} %get-tuple-element.7.r), custom_call_target="tpu_custom_call" | custom-call | tf_op jit(solution)/shard_map/put_out/pallas_call | solution.py:465
Async XLA Ops:
  0.6 0.8 %copy-start = (f32[16,768]{1,0:T(8,128)S(1)}, f32[16,768]{1,0:T(8,128)}, u32[]{:S(2)}) copy-start(f32[16,768]{1,0:T(8,128)} %d_hbm.1) | copy-start | bytes 147460

commit v4 on v3

--- a/solution.py
+++ b/solution.py
@@ -137,6 +137,13 @@
             carry = body(start + k, carry)
         return carry
     return lax.fori_loop(0, turns, turn, carry)
+
+
+def tree(terms):
+    while len(terms) > 1:
+        pairs = [terms[k] + terms[k + 1] for k in range(0, len(terms) - 1, 2)]
+        terms = pairs + terms[len(terms) - len(terms) % 2 :]
+    return terms[0]
 
 
 def wrap(i, n):
@@ -258,12 +265,10 @@
 
     tell(0)
 
+    hear(0)
+    tell(1)
     for copy in dens:
         copy.wait_recv()
-    for k in range(1, count):
-        if k == 1:
-            hear(0)
-            tell(1)
     for octet in range(4):
         x = sub + (8 * octet - 8)
         x_in = ((x >= 0) | (ix > 0)) & ((x < XC) | (ix < gxn - 1)) & live
@@ -296,17 +301,18 @@
     zero = jnp.zeros((LOADS, LANES), jnp.float32)
 
     def first_moment(x, s0):
+        terms = []
         for y in range(YC):
             r = rv[x + 2, y + 2]
-            s0 = s0 + r * (r * row_of(mi, y + 2, x + 8))
-        return s0
+            terms.append(r * (r * row_of(mi, y + 2, x + 8)))
+        return s0 + tree(terms)
 
     s0 = walk(0, XC, first_moment, zero, 2)
-    for copy in heat:
-        copy.wait_recv()
     for k in range(1, count - 1):
         hear(k)
         tell(k + 1)
+    for copy in heat:
+        copy.wait_recv()
 
     def scaled_row(i):
         out = []
@@ -326,16 +332,15 @@
     apply_rows(scaled_row, lambda i, y: row_of(cu, y + 1, i + 6), XN, emit_image, 0, BY_IMAGE)
 
     def emit_second(i, sums, extra):
-        s1, s2, s3 = extra
+        terms = [[], [], []]
         for y, off in enumerate(sums):
             q = qv[i, y + 1]
             yy = yv[i, y + 1]
             p = q + off
             pv[i - 1, y] = p
-            s1 = s1 + zv[i + 1, y + 2] * q
-            s2 = s2 + yy * q
-            s3 = s3 + yy * p
-        return s1, s2, s3
+            for some, term in zip(terms, (zv[i + 1, y + 2] * q, yy * q, yy * p)):
+                some.append(term)
+        return tuple(e + tree(t) for e, t in zip(extra, terms))
 
     moments = apply_rows(
         lambda i: [yv[i, y] for y in range(YC + 2)],
@@ -380,12 +385,9 @@
             copy.start()
         if step == len(groups) - 1:
             walk(0, XC, pack, 0, 2)
-        for copy in copies:
+        for copy in reversed(copies):
             copy.wait_recv()
-        total = rows[step]
-        for r in range(len(copies)):
-            total = total + got[done + r]
-        rows[step + 1] = total
+        rows[step + 1] = tree([rows[step]] + [got[done + r] for r in reversed(range(len(copies)))])
         done += len(copies)
         sent += copies
 
@@ -400,10 +402,12 @@
     for load in range(LOADS):
         f = jnp.broadcast_to(first[load : load + 1], (LOADS, LANES))
         m = jnp.broadcast_to(mu[load : load + 1], (LOADS, LANES))
-        for t in range(TILE_STEP // 8):
-            at = pl.ds(load * TILE_STEP + 8 * t, 8)
-            x_out[at, :] = f * zp[at, :] - m * yp[at, :]
-            r_out[at, :] = (hv[at, :] - f * qp[at, :]) + m * pp[at, :]
+        at = [pl.ds(load * TILE_STEP + 8 * t, 8) for t in range(TILE_STEP // 8)]
+        xs = [f * zp[a, :] - m * yp[a, :] for a in at]
+        rs = [(hv[a, :] - f * qp[a, :]) + m * pp[a, :] for a in at]
+        for a, x, r in zip(at, xs, rs):
+            x_out[a, :] = x
+            r_out[a, :] = r
     for copy in dens + heat + sent:
         copy.wait_send()
 

time: 42 us -> 41.2 us (0.981)
  Pallas kernels: 40.3 us -> 39.6 us
    pallas_call x1, Pallas kernels: 39.4 us -> 38.7 us  [per_device(): pl.pallas_call(functools.partial(kernel, gxn, lown, hin), out_shape=(out,...]
where the time goes in v4:
time: 41.2 us; the launch traced here: 41 us
  Pallas kernels  39.6 us (96%)
  local copies, waits for them, and re-layouts  0.79 us (2%)
  between operations  0.65 us (2%)
    pallas_call x1, Pallas kernels, per_device(): pl.pallas_call(functools.partial(kernel, gxn, lown, hin), out_shape=(out,...  38.7 us
    pallas_call x1, Pallas kernels, per_device(): pl.pallas_call(put_out, out_shape=(out, out), in_specs=[pl.BlockSpec(memo...  0.89 us

profile of v4, /device:TPU:1, one launch (start us, length us, event | category | flops | bytes accessed | tf_op | source)
XLA Modules:
  0.0 41.0 jit_solution(2939203566366855093)
XLA Ops:
  0.6 0.0 copy-start
  0.6 0.8 %copy-done = f32[16,768]{1,0:T(8,128)S(1)} copy-done((f32[16,768]{1,0:T(8,128)S(1)}, f32[16,768]{1,0:T(8,128)}, u32[]{:S(2)}) %copy-start) | copy-done | bytes 49176
  1.4 38.7 %two_steps.1 = (f32[768,128]{1,0:T(8,128)S(1)}, f32[768,128]{1,0:T(8,128)S(1)}) custom-call(f32[768,128]{1,0:T(8,128)} %bitcast.15, f32[16,768]{1,0:T(8,128)S(1)} %copy-done), custom_call_target="tpu_custom_call" | custom-call | tf_op jit(solution)/shard_map/two_steps/pallas_call | solution.py:434
  40.1 0.9 %put_out.1 = (f32[768,128]{1,0:T(8,128)}, f32[768,128]{1,0:T(8,128)}) custom-call(f32[768,128]{1,0:T(8,128)S(1)} %get-tuple-element.6.x, f32[768,128]{1,0:T(8,128)S(1)} %get-tuple-element.7.r), custom_call_target="tpu_custom_call" | custom-call | tf_op jit(solution)/shard_map/put_out/pallas_call | solution.py:469
Async XLA Ops:
  0.6 0.8 %copy-start = (f32[16,768]{1,0:T(8,128)S(1)}, f32[16,768]{1,0:T(8,128)}, u32[]{:S(2)}) copy-start(f32[16,768]{1,0:T(8,128)} %d_hbm.1) | copy-start | bytes 147460

commit v5 on v4

--- a/solution.py
+++ b/solution.py
@@ -24,6 +24,14 @@
 HEAT_TO = {1: (0, 2), 0: (2, XC), -1: (XC + 2, 2)}
 HEATY_FROM = {1: (YC, 2), 0: (2, YC), -1: (2, 2)}
 HEATY_TO = {1: (0, 2), 0: (2, YC), -1: (YC + 2, 2)}
+HALF = XC // 2
+HEAT_PARTS = (
+    [(0, dy, (2, HALF), (2, HALF)) for dy in (-1, 1)]
+    + [(1, dy, HEAT_FROM[1], HEAT_TO[1]) for dy in (0, -1, 1)]
+    + [(0, dy, (2 + HALF, HALF), (2 + HALF, HALF)) for dy in (-1, 1)]
+    + [(-1, dy, HEAT_FROM[-1], HEAT_TO[-1]) for dy in (0, -1, 1)]
+)
+EARLY = 5
 DENS_FROM = {1: (16, 8), 0: (8, 16), -1: (8, 8)}
 DENS_TO = {1: (0, 8), 0: (8, 16), -1: (24, 8)}
 DENSY_FROM = {1: (768, 384), 0: (384, 768), -1: (384, 256)}
@@ -32,6 +40,8 @@
 
 TILES = YC * NZ // LANES
 TILE_STEP = XC * TILES
+
+PARTS = [pl.ds(k * LOADS * TILE_STEP // 4, LOADS * TILE_STEP // 4) for k in range(4)]
 
 
 def to_tiles(field):
@@ -106,7 +116,7 @@
     return below, above
 
 
-def apply_rows(load_row, coef_at, rows, emit, start, by):
+def apply_rows(load_row, coef_at, rows, emit, start, by, between=None):
     first_row = row_fields(load_row(0))
     second = row_fields(load_row(1))
     _, above = element_row(first_row, second, lambda y: coef_at(0, y))
@@ -122,7 +132,11 @@
             sums.append((n_s + n_d) + pltpu.roll(n_s - n_d, 1, 1))
         return high, above, emit(i, sums, extra)
 
-    return walk(1, rows - 1, body, (second, above, start), by)[2]
+    carry, at = (second, above, start), 1
+    if between is not None:
+        carry, at = walk(1, 1 + by, body, carry, by), 1 + by
+        between()
+    return walk(at, rows - 1, body, carry, by)[2]
 
 
 def walk(start, stop, body, carry, by):
@@ -220,14 +234,16 @@
             if turn == k:
                 pl.semaphore_wait(known.at[at], 2)
 
-    take_d = pltpu.make_async_copy(d_hbm, dd.at[pl.ds(8, 16), pl.ds(384, 768)], in_sem.at[1])
-    take_h = pltpu.make_async_copy(h_hbm, hv, in_sem.at[0])
-    take_h.start()
+    take_d = pltpu.make_async_copy(d_hbm, dd.at[pl.ds(8, 16), pl.ds(384, 768)], in_sem.at[len(PARTS)])
+    take_h = [pltpu.make_async_copy(h_hbm.at[part], hv.at[part], in_sem.at[k]) for k, part in enumerate(PARTS)]
+    for copy in take_h:
+        copy.start()
     take_d.start()
     lane = lax.broadcasted_iota(jnp.int32, (LOADS, LANES), 1)
     sub = lax.broadcasted_iota(jnp.int32, (LOADS, LANES), 0)
     live = lane < NZ
-    take_h.wait()
+    for copy in take_h:
+        copy.wait()
 
     def lay_out(x, carry):
         tiles = [hv[pl.ds(tile_row(x, t), LOADS, stride=TILE_STEP), :] for t in range(6)]
@@ -251,13 +267,13 @@
         )
         copy.start()
         dens.append(copy)
-    for k, (dx, dy) in enumerate(SIDES):
+    for k, (dx, dy, from_x, to_x) in enumerate(HEAT_PARTS):
         copy = pltpu.make_async_remote_copy(
-            src_ref=rv.at[pl.ds(*HEAT_FROM[dx]), pl.ds(*HEATY_FROM[dy])],
-            dst_ref=rv.at[pl.ds(*HEAT_TO[dx]), pl.ds(*HEATY_TO[dy])],
+            src_ref=rv.at[pl.ds(*from_x), pl.ds(*HEATY_FROM[dy])],
+            dst_ref=rv.at[pl.ds(*to_x), pl.ds(*HEATY_TO[dy])],
             send_sem=heat_send.at[k],
             recv_sem=heat_recv.at[k],
-            device_id=beside[k],
+            device_id=beside[SIDES.index((dx, dy))],
             device_id_type=MESH,
         )
         copy.start()
@@ -311,8 +327,13 @@
     for k in range(1, count - 1):
         hear(k)
         tell(k + 1)
-    for copy in heat:
+    for copy in heat[:EARLY]:
         copy.wait_recv()
+
+    def wait_rest():
+        for copy in heat[EARLY:]:
+            copy.wait_recv()
+
 
     def scaled_row(i):
         out = []
@@ -329,7 +350,7 @@
             yv[i - 1, y] = q * row_of(mi, y + 1, i + 6)
         return extra
 
-    apply_rows(scaled_row, lambda i, y: row_of(cu, y + 1, i + 6), XN, emit_image, 0, BY_IMAGE)
+    apply_rows(scaled_row, lambda i, y: row_of(cu, y + 1, i + 6), XN, emit_image, 0, BY_IMAGE, wait_rest)
 
     def emit_second(i, sums, extra):
         terms = [[], [], []]
@@ -413,7 +434,11 @@
 
 
 def put_out(x, r, x_out, r_out, sem):
-    copies = [pltpu.make_async_copy(x, x_out, sem.at[0]), pltpu.make_async_copy(r, r_out, sem.at[1])]
+    copies = [
+        pltpu.make_async_copy(a.at[part], b.at[part], sem.at[i, k])
+        for k, part in enumerate(PARTS)
+        for i, (a, b) in enumerate(((x, x_out), (r, r_out)))
+    ]
     for copy in copies:
         copy.start()
     for copy in copies:
@@ -452,9 +477,9 @@
                 pltpu.VMEM((YN, 32, LANES), f32),
                 pltpu.VMEM((4, 1, LANES), f32),
                 pltpu.VMEM((count, 1, LANES), f32),
-                dma((2,)),
-                dma((8,)),
-                dma((8,)),
+                dma((len(PARTS) + 1,)),
+                dma((len(HEAT_PARTS),)),
+                dma((len(HEAT_PARTS),)),
                 dma((8,)),
                 dma((8,)),
                 dma((count,)),
@@ -471,7 +496,7 @@
             out_shape=(out, out),
             in_specs=[pl.BlockSpec(memory_space=pltpu.VMEM)] * 2,
             out_specs=[pl.BlockSpec(memory_space=pltpu.HBM)] * 2,
-            scratch_shapes=[dma((2,))],
+            scratch_shapes=[dma((2, len(PARTS)))],
             compiler_params=pltpu.CompilerParams(vmem_limit_bytes=2 * 1024 * 1024),
             name="put_out",
         )(sol, res)

time: 41.2 us -> 40.8 us (level)
  Pallas kernels: 39.6 us -> 39.1 us
    pallas_call x1, Pallas kernels: 38.7 us -> 38.2 us  [per_device(): pl.pallas_call(functools.partial(kernel, gxn, lown, hin), out_shape=(out,...]
where the time goes in v5:
time: 40.8 us; the launch traced here: 40.6 us
  Pallas kernels  39.1 us (96%)
  local copies, waits for them, and re-layouts  0.79 us (2%)
  between operations  0.65 us (2%)
    pallas_call x1, Pallas kernels, per_device(): pl.pallas_call(functools.partial(kernel, gxn, lown, hin), out_shape=(out,...  38.2 us
    pallas_call x1, Pallas kernels, per_device(): pl.pallas_call(put_out, out_shape=(out, out), in_specs=[pl.BlockSpec(memo...  0.94 us

profile of v5, /device:TPU:1, one launch (start us, length us, event | category | flops | bytes accessed | tf_op | source)
XLA Modules:
  0.0 40.6 jit_solution(1823913093994503460)
XLA Ops:
  0.6 0.0 copy-start
  0.6 0.8 %copy-done = f32[16,768]{1,0:T(8,128)S(1)} copy-done((f32[16,768]{1,0:T(8,128)S(1)}, f32[16,768]{1,0:T(8,128)}, u32[]{:S(2)}) %copy-start) | copy-done | bytes 49176
  1.4 38.2 %two_steps.1 = (f32[768,128]{1,0:T(8,128)S(1)}, f32[768,128]{1,0:T(8,128)S(1)}) custom-call(f32[768,128]{1,0:T(8,128)} %bitcast.15, f32[16,768]{1,0:T(8,128)S(1)} %copy-done), custom_call_target="tpu_custom_call" | custom-call | tf_op jit(solution)/shard_map/two_steps/pallas_call | solution.py:459
  39.6 0.9 %put_out.1 = (f32[768,128]{1,0:T(8,128)}, f32[768,128]{1,0:T(8,128)}) custom-call(f32[768,128]{1,0:T(8,128)S(1)} %get-tuple-element.6.x, f32[768,128]{1,0:T(8,128)S(1)} %get-tuple-element.7.r), custom_call_target="tpu_custom_call" | custom-call | tf_op jit(solution)/shard_map/put_out/pallas_call | solution.py:494
Async XLA Ops:
  0.6 0.8 %copy-start = (f32[16,768]{1,0:T(8,128)S(1)}, f32[16,768]{1,0:T(8,128)}, u32[]{:S(2)}) copy-start(f32[16,768]{1,0:T(8,128)} %d_hbm.1) | copy-start | bytes 147460

commit v6 on v5

--- a/solution.py
+++ b/solution.py
@@ -490,7 +490,7 @@
                 collective_id=0, has_side_effects=True, vmem_limit_bytes=GRANT
             ),
             name="two_steps",
-        )(to_tiles(heat_source), density)
+        )(to_tiles(heat_source), pltpu.with_memory_space_constraint(density, pltpu.HBM))
         sol, res = pl.pallas_call(
             put_out,
             out_shape=(out, out),

time: 40.8 us -> 39.9 us (0.978)
  local copies, waits for them, and re-layouts: 0.79 us -> 0 us
    unnamed x2 -> x0, local copies, waits for them, and re-layouts: 0.79 us -> none
where the time goes in v6:
time: 39.9 us; the launch traced here: 39.8 us
  Pallas kernels  39.1 us (98%)
  between operations  0.64 us (2%)
    pallas_call x1, Pallas kernels, per_device(): pl.pallas_call(functools.partial(kernel, gxn, lown, hin), out_shape=(out,...  38.2 us
    pallas_call x1, Pallas kernels, per_device(): pl.pallas_call(put_out, out_shape=(out, out), in_specs=[pl.BlockSpec(memo...  0.94 us

profile of v6, /device:TPU:1, one launch (start us, length us, event | category | flops | bytes accessed | tf_op | source)
XLA Modules:
  0.0 39.8 jit_solution(15693786274300515154)
XLA Ops:
  0.6 38.2 %two_steps.1 = (f32[768,128]{1,0:T(8,128)S(1)}, f32[768,128]{1,0:T(8,128)S(1)}) custom-call(f32[768,128]{1,0:T(8,128)} %bitcast.15, f32[16,768]{1,0:T(8,128)} %d_hbm.1), custom_call_target="tpu_custom_call" | custom-call | tf_op jit(solution)/shard_map/two_steps/pallas_call | solution.py:459
  38.8 0.9 %put_out.1 = (f32[768,128]{1,0:T(8,128)}, f32[768,128]{1,0:T(8,128)}) custom-call(f32[768,128]{1,0:T(8,128)S(1)} %get-tuple-element.6.x, f32[768,128]{1,0:T(8,128)S(1)} %get-tuple-element.7.r), custom_call_target="tpu_custom_call" | custom-call | tf_op jit(solution)/shard_map/put_out/pallas_call | solution.py:494
